TPU v7x, 128 devices: a whole 4x4x4 slice. The times are simulated.
128 devices in a mesh: blk: 16 (over x, z), beam: 8 (over y, core).
Axes of the slice: x: 4, y: 4, z: 4, core: 2. Of those that a mesh axis runs over, the one named last changes fastest.
Arguments:
- embeds: bfloat16 [4, 128, 2048], P(None, 'beam'), may hold values from -6 to 6
- attn_gain: float32 [2048], replicated, may hold values from 0.25 to 1.75
- w_query: bfloat16 [2048, 3072], P(None, 'blk'), may hold values from -0.125 to 0.125
- w_latent: bfloat16 [2048, 576], replicated, may hold values from -0.125 to 0.125
- latent_gain: float32 [512], replicated, may hold values from 0.3 to 3
- w_key_up: bfloat16 [16, 128, 512], P('blk'), may hold values from -0.5 to 0.5
- w_value_up: bfloat16 [16, 512, 128], P('blk'), may hold values from -0.25 to 0.25
- w_out: bfloat16 [2048, 2048], P('blk'), may hold values from -0.125 to 0.125
- ffn_gain: float32 [2048], replicated, may hold values from 0.25 to 1.75
- w_shared_gate: bfloat16 [2048, 2816], P(None, 'blk'), may hold values from -0.125 to 0.125
- w_shared_up: bfloat16 [2048, 2816], P(None, 'blk'), may hold values from -0.125 to 0.125
- w_shared_down: bfloat16 [2816, 2048], P('blk'), may hold values from -0.109375 to 0.109375
- w_expert_gate: bfloat16 [32, 2048, 2816], P('blk', None, 'beam'), may hold values from -0.125 to 0.125
- w_expert_up: bfloat16 [32, 2048, 2816], P('blk', None, 'beam'), may hold values from -0.125 to 0.125
- w_expert_down: bfloat16 [32, 2816, 2048], P('blk', 'beam'), may hold values from -0.15625 to 0.15625
- cache_pool: bfloat16 [16, 96, 128, 576], P('beam', 'blk'), may hold values from -1600 to 1600
- block_tables: int32 [16, 8, 64], P('beam'), may hold values from 0 to 95, as said below
- block_counts: int32 [16], P('beam'), may hold values from 4 to 64
- parents: int32 [4, 16, 8], P(None, 'beam'), may hold values from 0 to 7
- expert_ids: int32 [4, 128, 6], replicated, may hold values from 0 to 63, all different within a row; in each aligned block of 128 rows (0 to 127, 128 to 255, ..., all dimensions but the last counted through in order) at most 24 rows name the same one
- expert_weights: float32 [4, 128, 6], replicated, may hold values from 0.1 to 0.6
Outputs:
- layer_out: float32 [4, 128, 2048], P(None, ('blk', 'beam'))
Inputs may be any that keep to these rules, and one draw needn't show every extreme that they name: `block_tables`: for each group g, entries j below block_counts[g] of one beam name different physical blocks; entries at or beyond block_counts[g] are never read. `expert_ids`: the experts of one row differ; within one step all rows together name one expert at most 24 times.
All inputs are finite; a program needn't handle non-finite values.
Results may differ from a plain program's by a relative error of at most 0.034.
Values may be sent and summed in bfloat16 or wider, within the bound.
No kernel may reach another device: no remote copies, remote signals or barrier semaphores. Data moves between devices by JAX's collectives and lax.ppermute only.
A program may use at most 128 MiB of HBM per device.

v0:
```python
import jax
import jax.numpy as jnp
from jax import lax
from jax.sharding import PartitionSpec as P

EXPERTS = 64
FFE = 1408
THETA = 50000.0
EPS = 1e-06
NEG = -1e30


def combined_all(shard, axis, combine):
    everything = jax.tree.map(lambda part: lax.all_gather(part, axis), shard)
    initial = jax.tree.map(lambda part: part[0], everything)

    def step(k, so_far):
        return combine(so_far, jax.tree.map(lambda part: part[k], everything))

    return lax.fori_loop(1, lax.axis_size(axis), step, initial)


def rms_scale(values, gain):
    mean_sq = jnp.mean(values * values, axis=-1, keepdims=True)
    return values * lax.rsqrt(mean_sq + EPS) * gain


def rotate(values, position):
    half_dim = values.shape[-1] // 2
    frequency = THETA ** (-jnp.arange(half_dim, dtype=jnp.float32) * 2.0 / values.shape[-1])
    angles = position[..., None] * frequency
    cosine = jnp.cos(angles)
    sine_part = jnp.sin(angles)
    lower_half = values[..., :half_dim]
    upper_half = values[..., half_dim:]
    return jnp.concatenate(
        [
            lower_half * cosine - upper_half * sine_part,
            lower_half * sine_part + upper_half * cosine,
        ],
        axis=-1,
    )


def combine(earlier, later):
    top_first, sum_first, lat_first = earlier
    top_second, sum_second, lat_second = later
    top_score = jnp.maximum(top_first, top_second)
    scale_first = jnp.exp(top_first - top_score)
    scale_second = jnp.exp(top_second - top_score)
    return (
        top_score,
        sum_first * scale_first + sum_second * scale_second,
        lat_first * scale_first[..., None] + lat_second * scale_second[..., None],
    )


def partial_attend(scores, key_mask, values, form):
    masked = jnp.where(key_mask, scores, NEG)
    top_score = jnp.max(masked, axis=-1)
    weights = jnp.where(key_mask, jnp.exp(masked - top_score[..., None]), 0.0)
    weight_sum = jnp.sum(weights, axis=-1)
    latent_sum = jnp.einsum(
        form, weights.astype(jnp.bfloat16), values, preferred_element_type=jnp.float32
    )
    return (top_score, weight_sum, latent_sum)


def per_device(
    embeds,
    attn_gain,
    w_query,
    w_latent,
    latent_gain,
    w_key_up,
    w_value_up,
    w_out,
    ffn_gain,
    w_shared_gate,
    w_shared_up,
    w_shared_down,
    w_expert_gate,
    w_expert_up,
    w_expert_down,
    cache_pool,
    block_tables,
    block_counts,
    parents,
    expert_ids,
    expert_weights,
):
    step_count, row_dev, model_width = embeds.shape
    group_count, beam_count, max_blocks = block_tables.shape
    heads_dev, head_in, latent = w_key_up.shape
    entry_width = cache_pool.shape[3]
    pool_dev = cache_pool.shape[1]
    block_len = cache_pool.shape[2]
    value_dim = w_value_up.shape[2]
    pair_dev = w_expert_gate.shape[0]
    unit_dev = w_expert_gate.shape[2]
    topk_count = expert_ids.shape[2]
    blk_index = lax.axis_index("blk")
    beam_index = lax.axis_index("beam")
    total_rows = row_dev * lax.axis_size("beam")
    capacity = 2 * total_rows * topk_count // EXPERTS
    score_scale = (entry_width - latent + head_in) ** (-0.5)
    phys_ids = blk_index * pool_dev + jnp.arange(pool_dev, dtype=jnp.int32)
    cache_keys = cache_pool.reshape(group_count, pool_dev * block_len, entry_width)
    cache_values = cache_keys[:, :, :latent]
    recent = jnp.zeros((group_count, beam_count, step_count, entry_width), jnp.bfloat16)
    tables = block_tables
    base_pos = (block_counts * block_len).astype(jnp.float32)
    valid = jnp.arange(max_blocks, dtype=jnp.int32)[None, None, :] < block_counts[:, None, None]
    pair_half = beam_index * unit_dev // FFE
    local_experts = (blk_index * pair_dev + jnp.arange(pair_dev, dtype=jnp.int32)) * 2 + pair_half
    results = []
    for decode_step in range(step_count):
        parent = parents[decode_step]
        recent = jnp.take_along_axis(recent, parent[:, :, None, None], axis=1)
        tables = jnp.take_along_axis(tables, parent[:, :, None], axis=1)
        tokens = embeds[decode_step]
        normed = rms_scale(tokens.astype(jnp.float32), attn_gain).astype(jnp.bfloat16)
        queries = jnp.dot(normed, w_query, preferred_element_type=jnp.float32).astype(jnp.bfloat16)
        queries = queries.reshape(row_dev, heads_dev, w_query.shape[1] // heads_dev)
        position = jnp.repeat(base_pos + decode_step, beam_count)
        query_latent = jnp.einsum(
            "rhn,hnc->rhc", queries[:, :, :head_in], w_key_up, preferred_element_type=jnp.float32
        )
        query_rope = rotate(queries[:, :, head_in:].astype(jnp.float32), position[:, None])
        query_full = jnp.concatenate([query_latent, query_rope], axis=-1).astype(jnp.bfloat16)
        projected = jnp.dot(normed, w_latent, preferred_element_type=jnp.float32)
        new_entry = jnp.concatenate(
            [
                rms_scale(projected[:, :latent], latent_gain),
                rotate(projected[:, latent:], position),
            ],
            axis=-1,
        ).astype(jnp.bfloat16)
        recent = recent.at[:, :, decode_step].set(
            new_entry.reshape(group_count, beam_count, entry_width)
        )
        all_queries = lax.all_gather(query_full, "blk", axis=1, tiled=True)
        head_count = all_queries.shape[1]
        grouped = all_queries.reshape(group_count, beam_count * head_count, entry_width)
        scores = (
            jnp.einsum("gqe,gke->gqk", grouped, cache_keys, preferred_element_type=jnp.float32)
            * score_scale
        )
        block_used = (
            jnp.sum(
                ((tables[:, :, :, None] == phys_ids) & valid[..., None]).astype(jnp.int32), axis=2
            )
            > 0
        )
        key_mask = jnp.repeat(jnp.repeat(block_used, block_len, axis=2), head_count, axis=1)
        top_score, weight_sum, latent_sum = partial_attend(
            scores, key_mask, cache_values, "gqk,gkc->gqc"
        )
        top_score = top_score.reshape(row_dev, head_count)
        weight_sum = weight_sum.reshape(row_dev, head_count)
        latent_sum = latent_sum.reshape(row_dev, head_count, latent)
        merged = combined_all((top_score, weight_sum, latent_sum), "blk", combine)
        head_start = blk_index * heads_dev
        pooled = tuple(
            (lax.dynamic_slice_in_dim(member, head_start, heads_dev, 1) for member in merged)
        )
        recent_rows = recent.reshape(row_dev, step_count, entry_width)[:, : decode_step + 1]
        recent_scores = (
            jnp.einsum("rhe,rse->rhs", query_full, recent_rows, preferred_element_type=jnp.float32)
            * score_scale
        )
        recent_part = partial_attend(
            recent_scores,
            jnp.ones(recent_scores.shape, bool),
            recent_rows[:, :, :latent],
            "rhs,rsc->rhc",
        )
        top_score, weight_sum, latent_sum = combine(pooled, recent_part)
        attended = (latent_sum / weight_sum[..., None]).astype(jnp.bfloat16)
        head_out = jnp.einsum(
            "rhc,hcv->rhv", attended, w_value_up, preferred_element_type=jnp.float32
        ).astype(jnp.bfloat16)
        attn_part = jnp.dot(
            head_out.reshape(row_dev, heads_dev * value_dim),
            w_out,
            preferred_element_type=jnp.float32,
        )
        attn_total = lax.psum(attn_part, "blk")
        resid = tokens.astype(jnp.float32) + attn_total
        ffn_in = rms_scale(resid, ffn_gain).astype(jnp.bfloat16)
        all_rows = lax.all_gather(ffn_in, "beam", axis=0, tiled=True)
        matches = expert_ids[decode_step][:, :, None] == local_experts
        routed = jnp.any(matches, axis=1)
        row_weight = jnp.sum(
            jnp.where(matches, expert_weights[decode_step][:, :, None], 0.0), axis=1
        )
        slot_index = jnp.cumsum(routed.astype(jnp.int32), axis=0) - 1
        slot_index = jnp.where(routed, slot_index, capacity)
        expert_cols = jnp.broadcast_to(
            jnp.arange(pair_dev, dtype=jnp.int32)[None, :], (total_rows, pair_dev)
        )
        row_numbers = jnp.broadcast_to(
            jnp.arange(total_rows, dtype=jnp.int32)[:, None], (total_rows, pair_dev)
        )
        slot_rows = (
            jnp.full((pair_dev, capacity), total_rows, jnp.int32)
            .at[expert_cols, slot_index]
            .set(row_numbers, mode="drop")
        )
        weight_pad = jnp.concatenate([row_weight.T, jnp.zeros((pair_dev, 1), jnp.float32)], axis=1)
        slot_weight = jnp.take_along_axis(weight_pad, slot_rows, axis=1)
        picked = jnp.take(all_rows, slot_rows, axis=0, mode="fill", fill_value=0)
        gate_val = jnp.einsum(
            "ecd,edf->ecf", picked, w_expert_gate, preferred_element_type=jnp.float32
        )
        up_val = jnp.einsum("ecd,edf->ecf", picked, w_expert_up, preferred_element_type=jnp.float32)
        activation = (jax.nn.silu(gate_val) * up_val).astype(jnp.bfloat16)
        down_out = (
            jnp.einsum(
                "ecf,efd->ecd", activation, w_expert_down, preferred_element_type=jnp.float32
            )
            * slot_weight[..., None]
        )
        partial_term = (
            jnp.zeros((total_rows, model_width), jnp.float32)
            .at[slot_rows.reshape(-1)]
            .add(down_out.reshape(-1, model_width), mode="drop")
        )
        shared_act = (
            jax.nn.silu(jnp.dot(ffn_in, w_shared_gate, preferred_element_type=jnp.float32))
            * jnp.dot(ffn_in, w_shared_up, preferred_element_type=jnp.float32)
        ).astype(jnp.bfloat16)
        own_rows = jnp.dot(
            shared_act, w_shared_down, preferred_element_type=jnp.float32
        ) + jnp.where(blk_index == 0, resid, 0.0)
        row_start = beam_index * row_dev
        partial_term = lax.dynamic_update_slice_in_dim(
            partial_term,
            lax.dynamic_slice_in_dim(partial_term, row_start, row_dev, 0) + own_rows,
            row_start,
            0,
        )
        summed = lax.psum_scatter(partial_term, ("blk", "beam"), scatter_dimension=0, tiled=True)
        results.append(summed)
    return jnp.stack(results)


def solution(mesh):
    placed = (
        P(None, "beam", None),
        P(),
        P(None, "blk"),
        P(),
        P(),
        P("blk", None, None),
        P("blk", None, None),
        P("blk", None),
        P(),
        P(None, "blk"),
        P(None, "blk"),
        P("blk", None),
        P("blk", None, "beam"),
        P("blk", None, "beam"),
        P("blk", "beam", None),
        P("beam", "blk", None, None),
        P("beam", None, None),
        P("beam"),
        P(None, "beam", None),
        P(),
        P(),
    )
    return jax.shard_map(
        per_device,
        mesh=mesh,
        in_specs=placed,
        out_specs=P(None, ("blk", "beam"), None),
        check_vma=False,
    )
```

profile of v0, /device:TPU:1, one launch (start us, length us, event | category | flops | bytes accessed | tf_op | source)
XLA Modules:
  0.0 969.4 jit_solution(11336190134766764950)
XLA Ops:
  19.6 20.8 %all_gather.60 = bf16[16,16,576]{2,0,1:T(8,128)(2,1)S(1)} all-gather(bf16[16,1,576]{2,0,1:T(8,128)(2,1)S(1)} %pad_maximum_fusion.4), channel_id=1, replica_groups=mesh['blk'=16,'beam'=8] {'blk'}, dimensions={1}, use_global_device_ids=true | all-gather | bytes 313344 | tf_op jit(solution)/shard_map/all_gather | solution.py:142
  40.4 3.9 copy.230
  55.1 18.1 %all_gather.65 = bf16[16,16,576]{2,0,1:T(8,128)(2,1)S(1)} all-gather(bf16[16,1,576]{2,0,1:T(8,128)(2,1)S(1)} %pad_maximum_fusion.5), channel_id=1, replica_groups=mesh['blk'=16,'beam'=8] {'blk'}, dimensions={1}, use_global_device_ids=true | all-gather | bytes 313344 | tf_op jit(solution)/shard_map/all_gather | solution.py:142
  77.3 19.4 %all_gather.70 = bf16[16,16,576]{2,0,1:T(8,128)(2,1)S(1)} all-gather(bf16[16,1,576]{2,0,1:T(8,128)(2,1)S(1)} %pad_maximum_fusion.6), channel_id=1, replica_groups=mesh['blk'=16,'beam'=8] {'blk'}, dimensions={1}, use_global_device_ids=true | all-gather | bytes 313344 | tf_op jit(solution)/shard_map/all_gather | solution.py:142
  102.2 19.3 %all_gather.75 = bf16[16,16,576]{2,0,1:T(8,128)(2,1)S(1)} all-gather(bf16[16,1,576]{2,0,1:T(8,128)(2,1)S(1)} %pad_maximum_fusion.7), channel_id=1, replica_groups=mesh['blk'=16,'beam'=8] {'blk'}, dimensions={1}, use_global_device_ids=true | all-gather | bytes 313344 | tf_op jit(solution)/shard_map/all_gather | solution.py:142
  130.3 11.5 %scatter_fusion.3 = s32[2,24]{1,0:T(2,128)S(1)} fusion(s32[2,24]{1,0:T(2,128)S(1)} %broadcast.828.clone, s32[256]{0:T(256)S(1)} %reshape.1849, s32[256]{0:T(256)S(1)} %reshape.1809), kind=kCustom, calls=%fused_computation.22 | custom fusion | bytes 5120 | tf_op jit(solution)/shard_map/scatter | solution.py:208
  158.6 11.5 %scatter_fusion.2 = s32[2,24]{1,0:T(2,128)S(1)} fusion(s32[2,24]{1,0:T(2,128)S(1)} %broadcast.828.clone.1, s32[256]{0:T(256)S(1)} %reshape.1835, s32[256]{0:T(256)S(1)} %reshape.1809), kind=kCustom, calls=%fused_computation.20 | custom fusion | bytes 5120 | tf_op jit(solution)/shard_map/scatter | solution.py:208
  175.3 11.5 %scatter_fusion.1 = s32[2,24]{1,0:T(2,128)S(1)} fusion(s32[2,24]{1,0:T(2,128)S(1)} %broadcast.828.clone.2, s32[256]{0:T(256)S(1)} %reshape.1821, s32[256]{0:T(256)S(1)} %reshape.1809), kind=kCustom, calls=%fused_computation.18 | custom fusion | bytes 5120 | tf_op jit(solution)/shard_map/scatter | solution.py:208
  192.1 11.5 %scatter_fusion = s32[2,24]{1,0:T(2,128)S(1)} fusion(s32[2,24]{1,0:T(2,128)S(1)} %broadcast.828.clone.3, s32[256]{0:T(256)S(1)} %reshape.1807, s32[256]{0:T(256)S(1)} %reshape.1809), kind=kCustom, calls=%fused_computation.16 | custom fusion | bytes 5120 | tf_op jit(solution)/shard_map/scatter | solution.py:208
  209.0 19.1 %all_gather.61 = f32[16,16,16]{2,1,0:T(8,128)S(1)} all-gather(f32[1,16,16]{2,1,0:T(8,128)S(1)} %all_gather_reshape.36), channel_id=1, replica_groups=mesh['blk'=16,'beam'=8] {'blk'}, dimensions={0}, use_global_device_ids=true | all-gather | bytes 17408 | tf_op jit(solution)/shard_map/all_gather | solution.py:14
  228.2 18.1 %all_gather.62 = f32[16,16,16]{2,1,0:T(8,128)S(1)} all-gather(f32[1,16,16]{2,1,0:T(8,128)S(1)} %all_gather_reshape.37), channel_id=1, replica_groups=mesh['blk'=16,'beam'=8] {'blk'}, dimensions={0}, use_global_device_ids=true | all-gather | bytes 17408 | tf_op jit(solution)/shard_map/all_gather | solution.py:14
  252.9 19.4 %all_gather.66 = f32[16,16,16]{2,1,0:T(8,128)S(1)} all-gather(f32[1,16,16]{2,1,0:T(8,128)S(1)} %all_gather_reshape.39), channel_id=1, replica_groups=mesh['blk'=16,'beam'=8] {'blk'}, dimensions={0}, use_global_device_ids=true | all-gather | bytes 17408 | tf_op jit(solution)/shard_map/all_gather | solution.py:14
  273.0 16.5 %all_gather.67 = f32[16,16,16]{2,1,0:T(8,128)S(1)} all-gather(f32[1,16,16]{2,1,0:T(8,128)S(1)} %all_gather_reshape.40), channel_id=1, replica_groups=mesh['blk'=16,'beam'=8] {'blk'}, dimensions={0}, use_global_device_ids=true | all-gather | bytes 17408 | tf_op jit(solution)/shard_map/all_gather | solution.py:14
  295.8 18.2 %all_gather.71 = f32[16,16,16]{2,1,0:T(8,128)S(1)} all-gather(f32[1,16,16]{2,1,0:T(8,128)S(1)} %all_gather_reshape.42), channel_id=1, replica_groups=mesh['blk'=16,'beam'=8] {'blk'}, dimensions={0}, use_global_device_ids=true | all-gather | bytes 17408 | tf_op jit(solution)/shard_map/all_gather | solution.py:14
  314.8 18.2 %all_gather.72 = f32[16,16,16]{2,1,0:T(8,128)S(1)} all-gather(f32[1,16,16]{2,1,0:T(8,128)S(1)} %all_gather_reshape.43), channel_id=1, replica_groups=mesh['blk'=16,'beam'=8] {'blk'}, dimensions={0}, use_global_device_ids=true | all-gather | bytes 17408 | tf_op jit(solution)/shard_map/all_gather | solution.py:14
  338.0 18.5 %all_gather.76 = f32[16,16,16]{2,1,0:T(8,128)S(1)} all-gather(f32[1,16,16]{2,1,0:T(8,128)} %all_gather_reshape.45), channel_id=1, replica_groups=mesh['blk'=16,'beam'=8] {'blk'}, dimensions={0}, use_global_device_ids=true | all-gather | bytes 17408 | tf_op jit(solution)/shard_map/all_gather | solution.py:14
  357.3 15.7 %all_gather.77 = f32[16,16,16]{2,1,0:T(8,128)S(1)} all-gather(f32[1,16,16]{2,1,0:T(8,128)S(1)} %all_gather_reshape.46), channel_id=1, replica_groups=mesh['blk'=16,'beam'=8] {'blk'}, dimensions={0}, use_global_device_ids=true | all-gather | bytes 17408 | tf_op jit(solution)/shard_map/all_gather | solution.py:14
  390.7 29.7 %while.80 = (s32[]{:T(128)}, f32[16,16]{1,0:T(8,128)S(1)}, f32[16,16]{1,0:T(8,128)S(1)}, f32[16,16,512]{2,1,0:T(8,128)S(1)}, f32[16,16,16]{2,1,0:T(8,128)}, /*in...) while((s32[]{:T(128)}, f32[16,16]{1,0:T(8,128)S(1)}, ...), condition=%wide.region_8.10_spmd, body=%wide.region_7.9_spmd.sunk | while | flops 394757 | bytes 1583255 | solution.py:20
  423.9 29.6 %while.81 = (s32[]{:T(128)}, f32[16,16]{1,0:T(8,128)S(1)}, f32[16,16]{1,0:T(8,128)S(1)}, f32[16,16,512]{2,1,0:T(8,128)S(1)}, f32[16,16,16]{2,1,0:T(8,128)}, /*in...) while((s32[]{:T(128)}, f32[16,16]{1,0:T(8,128)S(1)}, ...), condition=%wide.region_23.28_spmd, body=%wide.region_22.27_spmd.sunk | while | flops 394757 | bytes 1583255 | solution.py:20
  457.2 29.6 %while.82 = (s32[]{:T(128)}, f32[16,16]{1,0:T(8,128)S(1)}, f32[16,16]{1,0:T(8,128)S(1)}, f32[16,16,512]{2,1,0:T(8,128)S(1)}, f32[16,16,16]{2,1,0:T(8,128)}, /*in...) while((s32[]{:T(128)}, f32[16,16]{1,0:T(8,128)S(1)}, ...), condition=%wide.region_40.45_spmd, body=%wide.region_39.44_spmd.sunk | while | flops 394757 | bytes 1583255 | solution.py:20
  490.4 38.8 %while.83 = (s32[]{:T(128)}, f32[16,16]{1,0:T(8,128)S(1)}, f32[16,16]{1,0:T(8,128)}, f32[16,16,512]{2,1,0:T(8,128)S(1)}, f32[16,16,16]{2,1,0:T(8,128)}, /*index=...) while((s32[]{:T(128)}, f32[16,16]{1,0:T(8,128)S(1)}, ...), condition=%wide.region_57.62_spmd, body=%wide.region_56.61_spmd.sunk | while | flops 394757 | bytes 1583255 | solution.py:20
  544.6 134.9 %all-reduce.15.cloned.1.call-done = (f32[16,2048]{1,0:T(8,128)}, f32[16,2048]{1,0:T(8,128)}, f32[16,2048]{1,0:T(8,128)}, f32[16,2048]{1,0:T(8,128)}) async-done(((f32[16,2048]{1,0:T(8,128)}, f32[16,2048]{1,0:T(8,128)}, f32[16,2048]{1,0:T(8,128)}, f32[16,2048]{1,0:T(8,128)}), (f32[16,2048]{1,0:T(8,128)}, f32[16,2048]{1,0:T(8,128)}, f32[16,2048]{1,0:T(8,128)}, ...) | async-done | bytes 524304 | tf_op jit(solution)/shard_map/psum | solution.py:188
  682.2 16.4 %all_gather.79 = bf16[128,2048]{1,0:T(8,128)(2,1)} all-gather(bf16[16,2048]{1,0:T(8,128)(2,1)S(1)} %get-tuple-element.895), channel_id=1, replica_groups=mesh['blk'=16,'beam'=8] {'beam'}, dimensions={0}, use_global_device_ids=true | all-gather | bytes 589824 | tf_op jit(solution)/shard_map/all_gather | solution.py:191
  700.7 14.3 %all_gather.74 = bf16[128,2048]{1,0:T(8,128)(2,1)} all-gather(bf16[16,2048]{1,0:T(8,128)(2,1)S(1)} %get-tuple-element.894), channel_id=1, replica_groups=mesh['blk'=16,'beam'=8] {'beam'}, dimensions={0}, use_global_device_ids=true | all-gather | bytes 589824 | tf_op jit(solution)/shard_map/all_gather | solution.py:191
  715.9 14.3 %all_gather.69 = bf16[128,2048]{1,0:T(8,128)(2,1)} all-gather(bf16[16,2048]{1,0:T(8,128)(2,1)S(1)} %get-tuple-element.893), channel_id=1, replica_groups=mesh['blk'=16,'beam'=8] {'beam'}, dimensions={0}, use_global_device_ids=true | all-gather | bytes 589824 | tf_op jit(solution)/shard_map/all_gather | solution.py:191
  731.1 14.2 %all_gather.64 = bf16[128,2048]{1,0:T(8,128)(2,1)} all-gather(bf16[16,2048]{1,0:T(8,128)(2,1)S(1)} %get-tuple-element.892), channel_id=1, replica_groups=mesh['blk'=16,'beam'=8] {'beam'}, dimensions={0}, use_global_device_ids=true | all-gather | bytes 589824 | tf_op jit(solution)/shard_map/all_gather | solution.py:191
  751.1 3.9 convolution_multiply_fusion
  759.7 3.4 fusion.66
  763.1 3.9 convolution_multiply_fusion.1
  780.7 3.9 convolution_multiply_fusion.2
  795.5 3.9 convolution_multiply_fusion.3
  804.8 153.5 %all-reduce.13.cloned.1.call-done = (f32[128,2048]{1,0:T(8,128)}, f32[128,2048]{1,0:T(8,128)}, f32[128,2048]{1,0:T(8,128)}, f32[128,2048]{1,0:T(8,128)}) async-done(((f32[128,2048]{1,0:T(8,128)}, f32[128,2048]{1,0:T(8,128)}, f32[128,2048]{1,0:T(8,128)}, f32[128,2048]{1,0:T(8,128)}), (f32[128,2048]{1,0:T(8,128)}, f32[128,2048]{1,0:T(8,128)}, f32[128,2048]{1,0:T(8,128)}, ...) | async-done | bytes 4194320
  (616 shorter events, 314.7 us)
Async XLA Ops:
  6.5 744.5 %copy-start = (bf16[2,352,2048]{2,1,0:T(8,128)(2,1)S(1)}, bf16[2,352,2048]{2,1,0:T(8,128)(2,1)}, u32[]{:S(2)}) copy-start(bf16[2,352,2048]{2,1,0:T(8,128)(2,1)} %param.59) | copy-start | bytes 8650756
  6.5 383.1 %all-gather.5.cloned.1.call-start = ((), (), s32[]{:S(2)}) async-start(), calls=%async_computation | async-start | bytes 8912896 | tf_op jit(solution)/shard_map/all_gather | solution.py:14
  49.0 373.9 %all-gather.7.cloned.1.call-start = ((), (), s32[]{:S(2)}) async-start(), calls=%async_computation.1 | async-start | bytes 8912896 | tf_op jit(solution)/shard_map/all_gather | solution.py:14
  54.4 47.2 %copy-start.49 = (bf16[16,1,32]{2,0,1:T(8,128)(2,1)}, bf16[16,1,32]{2,0,1:T(8,128)(2,1)S(1)}, u32[]{:S(2)}) copy-start(bf16[16,1,32]{2,0,1:T(8,128)(2,1)S(1)} %get-tuple-element.912) | copy-start | bytes 3076
  54.4 47.2 %copy-start.51 = (bf16[16,1,32]{2,0,1:T(8,128)(2,1)}, bf16[16,1,32]{2,0,1:T(8,128)(2,1)S(1)}, u32[]{:S(2)}) copy-start(bf16[16,1,32]{2,0,1:T(8,128)(2,1)S(1)} %get-tuple-element.913) | copy-start | bytes 3076
  76.5 379.6 %all-gather.9.cloned.1.call-start = ((), (), s32[]{:S(2)}) async-start(), calls=%async_computation.2 | async-start | bytes 8912896 | tf_op jit(solution)/shard_map/all_gather | solution.py:14
  101.4 387.8 %all-gather.11.cloned.1.call-start = ((), (), s32[]{:S(2)}) async-start(), calls=%async_computation.3 | async-start | bytes 8912896 | tf_op jit(solution)/shard_map/all_gather | solution.py:14
  126.3 553.2 %all-reduce.15.cloned.1.call-start = ((), (), s32[]{:S(2)}) async-start(), calls=%async_computation.5 | async-start | bytes 1048576 | tf_op jit(solution)/shard_map/psum | solution.py:188
  192.1 54.2 %copy-start.29 = (bf16[16,512]{1,0:T(8,128)(2,1)S(1)}, bf16[16,512]{1,0:T(8,128)(2,1)}, u32[]{:S(2)}) copy-start(bf16[16,512]{1,0:T(8,128)(2,1)} %copy-done.28) | copy-start | bytes 49156
  192.1 54.2 %copy-start.46 = (bf16[16,1,32]{2,0,1:T(8,128)(2,1)S(1)}, bf16[16,1,32]{2,0,1:T(8,128)(2,1)}, u32[]{:S(2)}) copy-start(bf16[16,1,32]{2,0,1:T(8,128)(2,1)} %copy-done.45) | copy-start | bytes 3076
  192.1 54.2 %copy-start.48 = (bf16[16,1,32]{2,0,1:T(8,128)(2,1)S(1)}, bf16[16,1,32]{2,0,1:T(8,128)(2,1)}, u32[]{:S(2)}) copy-start(bf16[16,1,32]{2,0,1:T(8,128)(2,1)} %copy-done.47) | copy-start | bytes 3076
  192.1 58.9 %copy-start.35 = (bf16[16,512]{1,0:T(8,128)(2,1)S(1)}, bf16[16,512]{1,0:T(8,128)(2,1)}, u32[]{:S(2)}) copy-start(bf16[16,512]{1,0:T(8,128)(2,1)} %copy-done.34) | copy-start | bytes 49156
  192.1 58.9 %copy-start.58 = (bf16[16,1,32]{2,0,1:T(8,128)(2,1)S(1)}, bf16[16,1,32]{2,0,1:T(8,128)(2,1)}, u32[]{:S(2)}) copy-start(bf16[16,1,32]{2,0,1:T(8,128)(2,1)} %copy-done.57) | copy-start | bytes 3076
  192.1 58.9 %copy-start.60 = (bf16[16,1,32]{2,0,1:T(8,128)(2,1)S(1)}, bf16[16,1,32]{2,0,1:T(8,128)(2,1)}, u32[]{:S(2)}) copy-start(bf16[16,1,32]{2,0,1:T(8,128)(2,1)} %copy-done.59) | copy-start | bytes 3076
  203.6 90.4 %copy-start.33 = (bf16[16,512]{1,0:T(8,128)(2,1)S(1)}, bf16[16,512]{1,0:T(8,128)(2,1)}, u32[]{:S(2)}) copy-start(bf16[16,512]{1,0:T(8,128)(2,1)} %copy-done.32) | copy-start | bytes 49156
  203.6 90.4 %copy-start.54 = (bf16[16,1,32]{2,0,1:T(8,128)(2,1)S(1)}, bf16[16,1,32]{2,0,1:T(8,128)(2,1)}, u32[]{:S(2)}) copy-start(bf16[16,1,32]{2,0,1:T(8,128)(2,1)} %copy-done.53) | copy-start | bytes 3076
  203.6 90.4 %copy-start.56 = (bf16[16,1,32]{2,0,1:T(8,128)(2,1)S(1)}, bf16[16,1,32]{2,0,1:T(8,128)(2,1)}, u32[]{:S(2)}) copy-start(bf16[16,1,32]{2,0,1:T(8,128)(2,1)} %copy-done.55) | copy-start | bytes 3076
  203.6 132.3 %copy-start.31 = (bf16[16,512]{1,0:T(8,128)(2,1)S(1)}, bf16[16,512]{1,0:T(8,128)(2,1)}, u32[]{:S(2)}) copy-start(bf16[16,512]{1,0:T(8,128)(2,1)} %copy-done.30) | copy-start | bytes 49156
  203.6 132.3 %copy-start.50 = (bf16[16,1,32]{2,0,1:T(8,128)(2,1)S(1)}, bf16[16,1,32]{2,0,1:T(8,128)(2,1)}, u32[]{:S(2)}) copy-start(bf16[16,1,32]{2,0,1:T(8,128)(2,1)} %copy-done.49) | copy-start | bytes 3076
  203.6 132.3 %copy-start.52 = (bf16[16,1,32]{2,0,1:T(8,128)(2,1)S(1)}, bf16[16,1,32]{2,0,1:T(8,128)(2,1)}, u32[]{:S(2)}) copy-start(bf16[16,1,32]{2,0,1:T(8,128)(2,1)} %copy-done.51) | copy-start | bytes 3076
  273.0 111.9 %copy-start.81 = (s32[2,24]{1,0:T(2,128)S(1)}, s32[2,24]{1,0:T(2,128)}, u32[]{:S(2)}) copy-start(s32[2,24]{1,0:T(2,128)} %compare_select_fusion.13) | copy-start | bytes 580
  273.0 113.7 %copy-start.67 = (f32[128,2]{0,1:T(2,128)S(1)}, f32[128,2]{0,1:T(2,128)}, u32[]{:S(2)}) copy-start(f32[128,2]{0,1:T(2,128)} %get-tuple-element.793) | copy-start | bytes 3076
  295.0 94.0 %copy-start.82 = (s32[2,24]{1,0:T(2,128)S(1)}, s32[2,24]{1,0:T(2,128)}, u32[]{:S(2)}) copy-start(s32[2,24]{1,0:T(2,128)} %compare_select_fusion.15) | copy-start | bytes 580
  333.0 56.6 %copy-start.23 = (f32[16,16,16]{2,1,0:T(8,128)}, f32[16,16,16]{2,1,0:T(8,128)S(1)}, u32[]{:S(2)}) copy-start(f32[16,16,16]{2,1,0:T(8,128)S(1)} %all_gather.72) | copy-start | bytes 49156
  490.3 43.5 %copy-start.10 = (bf16[1,512,128]{2,1,0:T(8,128)(2,1)S(1)}, bf16[1,512,128]{2,1,0:T(8,128)(2,1)}, u32[]{:S(2)}) copy-start(bf16[1,512,128]{2,1,0:T(8,128)(2,1)} %param.51) | copy-start | bytes 393220
  530.2 149.3 %copy-start.8 = (bf16[4,16,2048]{2,1,0:T(8,128)(2,1)S(1)}, bf16[4,16,2048]{2,1,0:T(8,128)(2,1)}, u32[]{:S(2)}) copy-start(bf16[4,16,2048]{2,1,0:T(8,128)(2,1)} %param.45) | copy-start | bytes 786436
  530.2 150.8 %copy-start.63 = (f32[2048]{0:T(1024)S(1)}, f32[2048]{0:T(1024)}, u32[]{:S(2)}) copy-start(f32[2048]{0:T(1024)} %param.53) | copy-start | bytes 24580
  542.2 416.1 %all-reduce.13.cloned.1.call-start = ((), (), s32[]{:S(2)}) async-start(), calls=%async_computation.4 | async-start | bytes 8388608
  682.2 63.1 %copy-start.15 = (bf16[16,2048]{1,0:T(8,128)(2,1)}, bf16[16,2048]{1,0:T(8,128)(2,1)S(1)}, u32[]{:S(2)}) copy-start(bf16[16,2048]{1,0:T(8,128)(2,1)S(1)} %get-tuple-element.893) | copy-start | bytes 196612
  682.2 63.1 %copy-start.16 = (bf16[16,2048]{1,0:T(8,128)(2,1)}, bf16[16,2048]{1,0:T(8,128)(2,1)S(1)}, u32[]{:S(2)}) copy-start(bf16[16,2048]{1,0:T(8,128)(2,1)S(1)} %get-tuple-element.894) | copy-start | bytes 196612
  682.2 63.1 %copy-start.18 = (bf16[16,2048]{1,0:T(8,128)(2,1)}, bf16[16,2048]{1,0:T(8,128)(2,1)S(1)}, u32[]{:S(2)}) copy-start(bf16[16,2048]{1,0:T(8,128)(2,1)S(1)} %get-tuple-element.895) | copy-start | bytes 196612
  700.7 47.7 %copy-start.76 = (pred[2,24]{1,0:T(4,128)(4,1)S(1)}, pred[2,24]{1,0:T(4,128)(4,1)}, u32[]{:S(2)}) copy-start(pred[2,24]{1,0:T(4,128)(4,1)} %compare_and_fusion) | copy-start | bytes 148
  (60 other events, 601.1 us)
Sparse Core Ops, SparseCore 0:
  49.1 78.4 all-gather.4
  129.8 70.4 all-gather.6
  202.5 71.7 all-gather.8
  276.2 71.4 all-gather.10
  542.4 137.1 all-reduce.14
  804.9 153.3 all-reduce.12
where the time goes:
time: 984 us; the launch traced here: 969 us
  waiting for transfers between devices  288 us (29%)
  blocking collectives  281 us (29%)
  other arithmetic  187 us (19%)
  local copies, waits for them, and re-layouts  113 us (11%)
  matrix products  82.2 us (8%)
  between operations  15.3 us (2%)
    unnamed x7, waiting for transfers between devices  154 us
    all_gather x8, blocking collectives, combined_all(): everything = jax.tree.map(lambda part: lax.all_gather(part, axis), shard)  144 us
    psum x1, waiting for transfers between devices, per_device(): attn_total = lax.psum(attn_part, 'blk')  135 us
    all_gather x4, blocking collectives, per_device(): all_queries = lax.all_gather(query_full, 'blk', axis=1, tiled=True)  77.6 us
    add x60, other arithmetic, combine(): lat_first * scale_first[..., None] + lat_second * scale_second[..., None]  72.7 us
    all_gather x4, blocking collectives, per_device(): all_rows = lax.all_gather(ffn_in, 'beam', axis=0, tiled=True)  59.2 us
    add x60, other arithmetic, combine(): sum_first * scale_first + sum_second * scale_second  53.2 us
    scatter x4, local copies, waits for them, and re-layouts, per_device(): slot_rows = jnp.full((pair_dev, capacity), total_rows, jnp.int32).at[expe...  45.8 us
  transfers between devices with their start and end apart: 6, of which 2 were waited for; matrix products, arithmetic and copies ran while one was open for 24% of the time, Pallas kernels for 0%

commit v1 on v0

--- a/solution.py
+++ b/solution.py
@@ -185,7 +185,11 @@
             w_out,
             preferred_element_type=jnp.float32,
         )
-        attn_total = lax.psum(attn_part, "blk")
+        attn_total = attn_part
+        for hop in (1, 2, 4, 8):
+            attn_total = attn_total + lax.ppermute(
+                attn_total, "blk", [(dev, dev ^ hop) for dev in range(16)]
+            )
         resid = tokens.astype(jnp.float32) + attn_total
         ffn_in = rms_scale(resid, ffn_gain).astype(jnp.bfloat16)
         all_rows = lax.all_gather(ffn_in, "beam", axis=0, tiled=True)

time: 984 us -> 937 us (0.952)
  waiting for transfers between devices: 288 us -> 156 us
  blocking collectives: 281 us -> 335 us
  other arithmetic: 187 us -> 207 us
  starting transfers between devices: 0.38 us -> 19.5 us
    psum x1 -> x0, waiting for transfers between devices: 135 us -> none  [per_device(): attn_total = lax.psum(attn_part, 'blk')]
    all_gather x4, blocking collectives: 59.2 us -> 113 us  [per_device(): all_rows = lax.all_gather(ffn_in, 'beam', axis=0, tiled=True)]
    add x60, other arithmetic: 53.2 us -> 72.4 us  [combine(): sum_first * scale_first + sum_second * scale_second]
    ppermute x0 -> x16, starting transfers between devices: none -> 19.2 us  [per_device(): lax.ppermute(attn_total, 'blk', [(dev, dev ^ hop) for dev in range(16)])]
    unnamed x7 -> x6, waiting for transfers between devices: 154 us -> 153 us
  transfers between devices with their start and end apart: 6 -> 21, of which waited for: 2 -> 2; matrix products, arithmetic and copies ran while one was open for 24% -> 32% of each run, Pallas kernels for 0% -> 0%
where the time goes in v1:
time: 937 us; the launch traced here: 923 us
  blocking collectives  335 us (36%)
  other arithmetic  207 us (22%)
  waiting for transfers between devices  156 us (17%)
  local copies, waits for them, and re-layouts  108 us (12%)
  matrix products  81.7 us (9%)
  starting transfers between devices  19.5 us (2%)
  between operations  15.3 us (2%)
    unnamed x6, waiting for transfers between devices  153 us
    all_gather x8, blocking collectives, combined_all(): everything = jax.tree.map(lambda part: lax.all_gather(part, axis), shard)  144 us
    all_gather x4, blocking collectives, per_device(): all_rows = lax.all_gather(ffn_in, 'beam', axis=0, tiled=True)  113 us
    all_gather x4, blocking collectives, per_device(): all_queries = lax.all_gather(query_full, 'blk', axis=1, tiled=True)  77.3 us
    add x60, other arithmetic, combine(): lat_first * scale_first[..., None] + lat_second * scale_second[..., None]  72.4 us
    add x60, other arithmetic, combine(): sum_first * scale_first + sum_second * scale_second  72.4 us
    scatter x4, local copies, waits for them, and re-layouts, per_device(): slot_rows = jnp.full((pair_dev, capacity), total_rows, jnp.int32).at[expe...  45.8 us
    ppermute x16, starting transfers between devices, per_device(): lax.ppermute(attn_total, 'blk', [(dev, dev ^ hop) for dev in range(16)])  19.2 us
  transfers between devices with their start and end apart: 21, of which 2 were waited for; matrix products, arithmetic and copies ran while one was open for 32% of the time, Pallas kernels for 0%

profile of v1, /device:TPU:1, one launch (start us, length us, event | category | flops | bytes accessed | tf_op | source)
XLA Modules:
  0.0 922.8 jit_solution(4268031375788828202)
XLA Ops:
  22.7 20.8 %all_gather.60 = bf16[16,16,576]{2,0,1:T(8,128)(2,1)S(1)} all-gather(bf16[16,1,576]{2,0,1:T(8,128)(2,1)S(1)} %pad_maximum_fusion.4), channel_id=1, replica_groups=mesh['blk'=16,'beam'=8] {'blk'}, dimensions={1}, use_global_device_ids=true | all-gather | bytes 313344 | tf_op jit(solution)/shard_map/all_gather | solution.py:142
  44.3 3.9 copy.230
  55.6 18.1 %all_gather.65 = bf16[16,16,576]{2,0,1:T(8,128)(2,1)S(1)} all-gather(bf16[16,1,576]{2,0,1:T(8,128)(2,1)S(1)} %pad_maximum_fusion.5), channel_id=1, replica_groups=mesh['blk'=16,'beam'=8] {'blk'}, dimensions={1}, use_global_device_ids=true | all-gather | bytes 313344 | tf_op jit(solution)/shard_map/all_gather | solution.py:142
  79.2 18.8 %all_gather.70 = bf16[16,16,576]{2,0,1:T(8,128)(2,1)S(1)} all-gather(bf16[16,1,576]{2,0,1:T(8,128)(2,1)S(1)} %pad_maximum_fusion.6), channel_id=1, replica_groups=mesh['blk'=16,'beam'=8] {'blk'}, dimensions={1}, use_global_device_ids=true | all-gather | bytes 313344 | tf_op jit(solution)/shard_map/all_gather | solution.py:142
  103.6 19.6 %all_gather.75 = bf16[16,16,576]{2,0,1:T(8,128)(2,1)S(1)} all-gather(bf16[16,1,576]{2,0,1:T(8,128)(2,1)S(1)} %pad_maximum_fusion.7), channel_id=1, replica_groups=mesh['blk'=16,'beam'=8] {'blk'}, dimensions={1}, use_global_device_ids=true | all-gather | bytes 313344 | tf_op jit(solution)/shard_map/all_gather | solution.py:142
  132.1 11.5 %scatter_fusion.3 = s32[2,24]{1,0:T(2,128)S(1)} fusion(s32[2,24]{1,0:T(2,128)S(1)} %broadcast.828.clone, s32[256]{0:T(256)S(1)} %reshape.1849, s32[256]{0:T(256)S(1)} %reshape.1809), kind=kCustom, calls=%fused_computation.22 | custom fusion | bytes 5120 | tf_op jit(solution)/shard_map/scatter | solution.py:212
  157.2 11.5 %scatter_fusion.2 = s32[2,24]{1,0:T(2,128)S(1)} fusion(s32[2,24]{1,0:T(2,128)S(1)} %broadcast.828.clone.1, s32[256]{0:T(256)S(1)} %reshape.1835, s32[256]{0:T(256)S(1)} %reshape.1809), kind=kCustom, calls=%fused_computation.20 | custom fusion | bytes 5120 | tf_op jit(solution)/shard_map/scatter | solution.py:212
  172.8 11.5 %scatter_fusion.1 = s32[2,24]{1,0:T(2,128)S(1)} fusion(s32[2,24]{1,0:T(2,128)S(1)} %broadcast.828.clone.2, s32[256]{0:T(256)S(1)} %reshape.1821, s32[256]{0:T(256)S(1)} %reshape.1809), kind=kCustom, calls=%fused_computation.18 | custom fusion | bytes 5120 | tf_op jit(solution)/shard_map/scatter | solution.py:212
  189.1 11.5 %scatter_fusion = s32[2,24]{1,0:T(2,128)S(1)} fusion(s32[2,24]{1,0:T(2,128)S(1)} %broadcast.828.clone.3, s32[256]{0:T(256)S(1)} %reshape.1807, s32[256]{0:T(256)S(1)} %reshape.1809), kind=kCustom, calls=%fused_computation.16 | custom fusion | bytes 5120 | tf_op jit(solution)/shard_map/scatter | solution.py:212
  205.0 18.1 %all_gather.61 = f32[16,16,16]{2,1,0:T(8,128)S(1)} all-gather(f32[1,16,16]{2,1,0:T(8,128)S(1)} %all_gather_reshape.36), channel_id=1, replica_groups=mesh['blk'=16,'beam'=8] {'blk'}, dimensions={0}, use_global_device_ids=true | all-gather | bytes 17408 | tf_op jit(solution)/shard_map/all_gather | solution.py:14
  224.4 16.5 %all_gather.62 = f32[16,16,16]{2,1,0:T(8,128)S(1)} all-gather(f32[1,16,16]{2,1,0:T(8,128)S(1)} %all_gather_reshape.37), channel_id=1, replica_groups=mesh['blk'=16,'beam'=8] {'blk'}, dimensions={0}, use_global_device_ids=true | all-gather | bytes 17408 | tf_op jit(solution)/shard_map/all_gather | solution.py:14
  246.0 20.4 %all_gather.66 = f32[16,16,16]{2,1,0:T(8,128)S(1)} all-gather(f32[1,16,16]{2,1,0:T(8,128)S(1)} %all_gather_reshape.39), channel_id=1, replica_groups=mesh['blk'=16,'beam'=8] {'blk'}, dimensions={0}, use_global_device_ids=true | all-gather | bytes 17408 | tf_op jit(solution)/shard_map/all_gather | solution.py:14
  267.2 16.3 %all_gather.67 = f32[16,16,16]{2,1,0:T(8,128)S(1)} all-gather(f32[1,16,16]{2,1,0:T(8,128)S(1)} %all_gather_reshape.40), channel_id=1, replica_groups=mesh['blk'=16,'beam'=8] {'blk'}, dimensions={0}, use_global_device_ids=true | all-gather | bytes 17408 | tf_op jit(solution)/shard_map/all_gather | solution.py:14
  287.8 19.5 %all_gather.71 = f32[16,16,16]{2,1,0:T(8,128)S(1)} all-gather(f32[1,16,16]{2,1,0:T(8,128)S(1)} %all_gather_reshape.42), channel_id=1, replica_groups=mesh['blk'=16,'beam'=8] {'blk'}, dimensions={0}, use_global_device_ids=true | all-gather | bytes 17408 | tf_op jit(solution)/shard_map/all_gather | solution.py:14
  308.7 17.2 %all_gather.72 = f32[16,16,16]{2,1,0:T(8,128)S(1)} all-gather(f32[1,16,16]{2,1,0:T(8,128)S(1)} %all_gather_reshape.43), channel_id=1, replica_groups=mesh['blk'=16,'beam'=8] {'blk'}, dimensions={0}, use_global_device_ids=true | all-gather | bytes 17408 | tf_op jit(solution)/shard_map/all_gather | solution.py:14
  330.2 20.5 %all_gather.76 = f32[16,16,16]{2,1,0:T(8,128)S(1)} all-gather(f32[1,16,16]{2,1,0:T(8,128)S(1)} %all_gather_reshape.45), channel_id=1, replica_groups=mesh['blk'=16,'beam'=8] {'blk'}, dimensions={0}, use_global_device_ids=true | all-gather | bytes 17408 | tf_op jit(solution)/shard_map/all_gather | solution.py:14
  350.7 15.4 %all_gather.77 = f32[16,16,16]{2,1,0:T(8,128)S(1)} all-gather(f32[1,16,16]{2,1,0:T(8,128)S(1)} %all_gather_reshape.46), channel_id=1, replica_groups=mesh['blk'=16,'beam'=8] {'blk'}, dimensions={0}, use_global_device_ids=true | all-gather | bytes 17408 | tf_op jit(solution)/shard_map/all_gather | solution.py:14
  373.9 39.0 %while.80 = (s32[]{:T(128)}, f32[16,16]{1,0:T(8,128)}, f32[16,16]{1,0:T(8,128)}, f32[16,16,512]{2,1,0:T(8,128)S(1)}, f32[16,16,16]{2,1,0:T(8,128)}, /*index=5*/f...) while((s32[]{:T(128)}, f32[16,16]{1,0:T(8,128)}, ...), condition=%wide.region_8.10_spmd, body=%wide.region_7.9_spmd.sunk | while | flops 394757 | bytes 1583255 | solution.py:20
  421.3 38.9 %while.81 = (s32[]{:T(128)}, f32[16,16]{1,0:T(8,128)}, f32[16,16]{1,0:T(8,128)}, f32[16,16,512]{2,1,0:T(8,128)S(1)}, f32[16,16,16]{2,1,0:T(8,128)}, /*index=5*/f...) while((s32[]{:T(128)}, f32[16,16]{1,0:T(8,128)}, ...), condition=%wide.region_22.27_spmd, body=%wide.region_21.26_spmd.sunk | while | flops 394757 | bytes 1583255 | solution.py:20
  466.8 39.0 %while.82 = (s32[]{:T(128)}, f32[16,16]{1,0:T(8,128)}, f32[16,16]{1,0:T(8,128)}, f32[16,16,512]{2,1,0:T(8,128)S(1)}, f32[16,16,16]{2,1,0:T(8,128)}, /*index=5*/f...) while((s32[]{:T(128)}, f32[16,16]{1,0:T(8,128)}, ...), condition=%wide.region_38.43_spmd, body=%wide.region_37.42_spmd.sunk | while | flops 394757 | bytes 1583255 | solution.py:20
  513.8 29.6 %while.83 = (s32[]{:T(128)}, f32[16,16]{1,0:T(8,128)S(1)}, f32[16,16]{1,0:T(8,128)S(1)}, f32[16,16,512]{2,1,0:T(8,128)S(1)}, f32[16,16,16]{2,1,0:T(8,128)}, /*in...) while((s32[]{:T(128)}, f32[16,16]{1,0:T(8,128)S(1)}, ...), condition=%wide.region_54.59_spmd, body=%wide.region_53.58_spmd.sunk | while | flops 394757 | bytes 1583255 | solution.py:20
  581.8 71.8 %all_gather.79 = bf16[128,2048]{1,0:T(8,128)(2,1)} all-gather(bf16[16,2048]{1,0:T(8,128)(2,1)S(1)} %get-tuple-element.934), channel_id=1, replica_groups=mesh['blk'=16,'beam'=8] {'beam'}, dimensions={0}, use_global_device_ids=true | all-gather | bytes 589824 | tf_op jit(solution)/shard_map/all_gather | solution.py:195
  654.5 14.2 %all_gather.74 = bf16[128,2048]{1,0:T(8,128)(2,1)} all-gather(bf16[16,2048]{1,0:T(8,128)(2,1)S(1)} %get-tuple-element.933), channel_id=1, replica_groups=mesh['blk'=16,'beam'=8] {'beam'}, dimensions={0}, use_global_device_ids=true | all-gather | bytes 589824 | tf_op jit(solution)/shard_map/all_gather | solution.py:195
  669.6 14.2 %all_gather.69 = bf16[128,2048]{1,0:T(8,128)(2,1)} all-gather(bf16[16,2048]{1,0:T(8,128)(2,1)S(1)} %get-tuple-element.932), channel_id=1, replica_groups=mesh['blk'=16,'beam'=8] {'beam'}, dimensions={0}, use_global_device_ids=true | all-gather | bytes 589824 | tf_op jit(solution)/shard_map/all_gather | solution.py:195
  684.7 13.1 %all_gather.64 = bf16[128,2048]{1,0:T(8,128)(2,1)S(1)} all-gather(bf16[16,2048]{1,0:T(8,128)(2,1)S(1)} %get-tuple-element.931), channel_id=1, replica_groups=mesh['blk'=16,'beam'=8] {'beam'}, dimensions={0}, use_global_device_ids=true | all-gather | bytes 589824 | tf_op jit(solution)/shard_map/all_gather | solution.py:195
  700.9 3.5 fusion.63
  704.4 4.0 convolution_multiply_fusion
  717.3 4.1 convolution_multiply_fusion.1
  732.5 3.5 fusion.61
  736.0 4.0 convolution_multiply_fusion.2
  749.9 3.9 convolution_multiply_fusion.3
  759.1 152.6 %all-reduce.11.cloned.1.call-done = (f32[128,2048]{1,0:T(8,128)}, f32[128,2048]{1,0:T(8,128)}, f32[128,2048]{1,0:T(8,128)}, f32[128,2048]{1,0:T(8,128)}) async-done(((f32[128,2048]{1,0:T(8,128)}, f32[128,2048]{1,0:T(8,128)}, f32[128,2048]{1,0:T(8,128)}, f32[128,2048]{1,0:T(8,128)}), (f32[128,2048]{1,0:T(8,128)}, f32[128,2048]{1,0:T(8,128)}, f32[128,2048]{1,0:T(8,128)}, ...) | async-done | bytes 4194320
  (659 shorter events, 345.8 us)
Async XLA Ops:
  6.5 697.8 %copy-start = (bf16[2,352,2048]{2,1,0:T(8,128)(2,1)S(1)}, bf16[2,352,2048]{2,1,0:T(8,128)(2,1)}, u32[]{:S(2)}) copy-start(bf16[2,352,2048]{2,1,0:T(8,128)(2,1)} %param.59) | copy-start | bytes 8650756
  6.5 366.3 %all-gather.5.cloned.1.call-start = ((), (), s32[]{:S(2)}) async-start(), calls=%async_computation | async-start | bytes 8912896 | tf_op jit(solution)/shard_map/all_gather | solution.py:14
  53.0 367.3 %all-gather.7.cloned.1.call-start = ((), (), s32[]{:S(2)}) async-start(), calls=%async_computation.1 | async-start | bytes 8912896 | tf_op jit(solution)/shard_map/all_gather | solution.py:14
  78.4 387.3 %all-gather.9.cloned.1.call-start = ((), (), s32[]{:S(2)}) async-start(), calls=%async_computation.2 | async-start | bytes 8912896 | tf_op jit(solution)/shard_map/all_gather | solution.py:14
  102.8 409.9 %all-gather.11.cloned.1.call-start = ((), (), s32[]{:S(2)}) async-start(), calls=%async_computation.3 | async-start | bytes 8912896 | tf_op jit(solution)/shard_map/all_gather | solution.py:14
  128.0 783.7 %all-reduce.11.cloned.1.call-start = ((), (), s32[]{:S(2)}) async-start(), calls=%async_computation.4 | async-start | bytes 8388608
  200.6 108.0 %copy-start.71 = (f32[2,128]{1,0:T(2,128)S(1)}, f32[2,128]{1,0:T(2,128)}, u32[]{:S(2)}) copy-start(f32[2,128]{1,0:T(2,128)} %get-tuple-element.889) | copy-start | bytes 3076
  200.6 126.6 %copy-start.81 = (s32[2,8,1]{1,0,2:T(2,128)S(1)}, s32[2,8,1]{1,0,2:T(2,128)}, u32[]{:S(2)}) copy-start(s32[2,8,1]{1,0,2:T(2,128)} %get-tuple-element.943) | copy-start | bytes 196
  200.6 127.5 %copy-start.35 = (bf16[16,512]{1,0:T(8,128)(2,1)S(1)}, bf16[16,512]{1,0:T(8,128)(2,1)}, u32[]{:S(2)}) copy-start(bf16[16,512]{1,0:T(8,128)(2,1)} %copy-done.34) | copy-start | bytes 49156
  200.6 127.5 %copy-start.54 = (bf16[16,1,32]{2,0,1:T(8,128)(2,1)S(1)}, bf16[16,1,32]{2,0,1:T(8,128)(2,1)}, u32[]{:S(2)}) copy-start(bf16[16,1,32]{2,0,1:T(8,128)(2,1)} %copy-done.53) | copy-start | bytes 3076
  200.6 127.5 %copy-start.56 = (bf16[16,1,32]{2,0,1:T(8,128)(2,1)S(1)}, bf16[16,1,32]{2,0,1:T(8,128)(2,1)}, u32[]{:S(2)}) copy-start(bf16[16,1,32]{2,0,1:T(8,128)(2,1)} %copy-done.55) | copy-start | bytes 3076
  203.3 147.3 %copy-start.70 = (f32[2,128]{1,0:T(2,128)S(1)}, f32[2,128]{1,0:T(2,128)}, u32[]{:S(2)}) copy-start(f32[2,128]{1,0:T(2,128)} %get-tuple-element.891) | copy-start | bytes 3076
  418.4 129.6 %collective-permute-start = (f32[16,2048]{1,0:T(8,128)}, f32[16,2048]{1,0:T(8,128)}, u32[]{:S(2)}, u32[]{:S(2)}) collective-permute-start(f32[16,2048]{1,0:T(8,128)} %fusion.32), channel_id=1, source_target_pairs={{0,8},{8,0},{16,24},{24,16},{32,40},{40,32},{48,56},{56,48},{64,72... | collective-permute-start | bytes 393224 | tf_op jit(solution)/shard_map/ppermute | solution.py:190
  465.7 85.4 %collective-permute-start.4 = (f32[16,2048]{1,0:T(8,128)}, f32[16,2048]{1,0:T(8,128)}, u32[]{:S(2)}, u32[]{:S(2)}) collective-permute-start(f32[16,2048]{1,0:T(8,128)} %fusion.33), channel_id=1, source_target_pairs={{0,8},{8,0},{16,24},{24,16},{32,40},{40,32},{48,56},{56,48},{64,72... | collective-permute-start | bytes 393224 | tf_op jit(solution)/shard_map/ppermute | solution.py:190
  511.3 41.8 %collective-permute-start.8 = (f32[16,2048]{1,0:T(8,128)}, f32[16,2048]{1,0:T(8,128)}, u32[]{:S(2)}, u32[]{:S(2)}) collective-permute-start(f32[16,2048]{1,0:T(8,128)} %fusion.34), channel_id=1, source_target_pairs={{0,8},{8,0},{16,24},{24,16},{32,40},{40,32},{48,56},{56,48},{64,72... | collective-permute-start | bytes 393224 | tf_op jit(solution)/shard_map/ppermute | solution.py:190
  546.8 9.5 %collective-permute-start.12 = (f32[16,2048]{1,0:T(8,128)S(1)}, f32[16,2048]{1,0:T(8,128)S(1)}, u32[]{:S(2)}, u32[]{:S(2)}) collective-permute-start(f32[16,2048]{1,0:T(8,128)S(1)} %fusion.35), channel_id=1, source_target_pairs={{0,8},{8,0},{16,24},{24,16},{32,40},{40,32},{48,56},{56,48},{64,72... | collective-permute-start | bytes 393224 | tf_op jit(solution)/shard_map/ppermute | solution.py:190
  549.0 9.4 %collective-permute-start.1 = (f32[16,2048]{1,0:T(8,128)S(1)}, f32[16,2048]{1,0:T(8,128)S(1)}, u32[]{:S(2)}, u32[]{:S(2)}) collective-permute-start(f32[16,2048]{1,0:T(8,128)S(1)} %add.720), channel_id=1, source_target_pairs={{0,16},{8,24},{16,0},{24,8},{32,48},{40,56},{48,32},{56,40},{64,80... | collective-permute-start | bytes 393224 | tf_op jit(solution)/shard_map/ppermute | solution.py:190
  552.1 8.0 collective-permute-start.5
  554.1 6.2 collective-permute-start.9
  556.3 6.1 collective-permute-start.13
  558.4 6.0 collective-permute-start.2
  560.1 7.5 collective-permute-start.6
  560.9 8.5 collective-permute-start.10
  563.0 9.7 %collective-permute-start.14 = (f32[16,2048]{1,0:T(8,128)}, f32[16,2048]{1,0:T(8,128)}, u32[]{:S(2)}, u32[]{:S(2)}) collective-permute-start(f32[16,2048]{1,0:T(8,128)} %add.779), channel_id=1, source_target_pairs={{0,32},{8,40},{16,48},{24,56},{32,0},{40,8},{48,16},{56,24},{64,96... | collective-permute-start | bytes 393224 | tf_op jit(solution)/shard_map/ppermute | solution.py:190
  565.4 11.7 %collective-permute-start.3 = (f32[16,2048]{1,0:T(8,128)S(1)}, f32[16,2048]{1,0:T(8,128)}, u32[]{:S(2)}, u32[]{:S(2)}) collective-permute-start(f32[16,2048]{1,0:T(8,128)S(1)} %add.722), channel_id=1, source_target_pairs={{0,64},{8,72},{16,80},{24,88},{32,96},{40,104},{48,112},{56,120},{... | collective-permute-start | bytes 393224 | tf_op jit(solution)/shard_map/ppermute | solution.py:190
  568.6 8.5 collective-permute-start.7
  570.4 6.6 collective-permute-start.11
  574.4 5.6 collective-permute-start.15
  581.7 116.1 %copy-start.15 = (bf16[16,2048]{1,0:T(8,128)(2,1)}, bf16[16,2048]{1,0:T(8,128)(2,1)S(1)}, u32[]{:S(2)}) copy-start(bf16[16,2048]{1,0:T(8,128)(2,1)S(1)} %get-tuple-element.931) | copy-start | bytes 196612
  581.7 116.0 %copy-start.17 = (bf16[16,2048]{1,0:T(8,128)(2,1)}, bf16[16,2048]{1,0:T(8,128)(2,1)S(1)}, u32[]{:S(2)}) copy-start(bf16[16,2048]{1,0:T(8,128)(2,1)S(1)} %get-tuple-element.932) | copy-start | bytes 196612
  581.7 116.0 %copy-start.18 = (bf16[16,2048]{1,0:T(8,128)(2,1)}, bf16[16,2048]{1,0:T(8,128)(2,1)S(1)}, u32[]{:S(2)}) copy-start(bf16[16,2048]{1,0:T(8,128)(2,1)S(1)} %get-tuple-element.933) | copy-start | bytes 196612
  581.8 116.0 %copy-start.19 = (bf16[16,2048]{1,0:T(8,128)(2,1)}, bf16[16,2048]{1,0:T(8,128)(2,1)S(1)}, u32[]{:S(2)}) copy-start(bf16[16,2048]{1,0:T(8,128)(2,1)S(1)} %get-tuple-element.934) | copy-start | bytes 196612
  (76 other events, 2049.6 us)
Sparse Core Ops, SparseCore 0:
  53.1 78.2 all-gather.4
  133.6 70.4 all-gather.6
  206.2 71.4 all-gather.8
  279.7 71.8 all-gather.10
  759.2 152.4 all-reduce.10
